TPU v7x, 128 devices: a whole 4x4x4 slice. The times are simulated.
128 devices in a mesh: wide: 32 (over y, z, core), narrow: 4 (over x).
Axes of the slice: x: 4, y: 4, z: 4, core: 2. Of those that a mesh axis runs over, the one named last changes fastest.
Arguments:
- layer_input_rows: bfloat16 [65536, 4096], P('wide', 'narrow'), may hold values from -6 to 6
- output_gradient_rows: bfloat16 [65536, 4096], P('wide', 'narrow'), may hold values from -60 to 60
- adapter_up_weight: bfloat16 [4096, 128], P('narrow'), may hold values from -0.09375 to 0.09375
- input_side_projection: bfloat16 [4096, 128], P('narrow'), may hold values from -0.09375 to 0.09375
- rank_side_projection: bfloat16 [128, 64], replicated, may hold values from -6 to 6
- lengths: int32 [2048], P('wide'), may hold values from 1 to 32, 40960 in all
- program_output_index: int32 [2048], replicated, may hold values from 0 to 2047, each once
- targets: bfloat16 [65536, 8192], P('wide', 'narrow'), may hold values from -650 to 650
Outputs:
- scores: float32 [2048, 65536], P('narrow', 'wide')
Inputs may be any that keep to these rules, and one draw needn't show every extreme that they name: Program s uses its first lengths[s] token rows; some program uses all 32. `program_output_index`: each output row is named by exactly one program.
All inputs are finite; a program needn't handle non-finite values. No bound on the sum of `lengths` on one device may be relied on, other than what follows from the above.
Results may differ from a plain program's by a relative error of at most 0.025.
Values may be sent and summed in bfloat16 or wider, within the bound.
A program may use at most 128 MiB of HBM per device.

v0:
```python
import math
import jax
import jax.numpy as jnp
from jax import lax
from jax.sharding import PartitionSpec as P

epsilon = 1e-06


def program_features(out_side, in_side, lengths, length):
    programs = lengths.shape[0]
    positions = lax.broadcasted_iota(jnp.int32, (programs, length), 1)
    live_rows = (positions < lengths[:, None]).astype(jnp.float32)
    weighted = out_side.reshape(programs, length, -1) * live_rows[:, :, None]
    inputs = in_side.reshape(programs, length, -1)
    outer_sum = jnp.einsum("sla,slb->sab", weighted, inputs, precision=lax.Precision.HIGHEST)
    return outer_sum.reshape(programs, -1)


def normalize_rows(features, squares):
    return (features * lax.rsqrt(squares + epsilon)[:, None]).astype(jnp.bfloat16)


def shards(
    layer_input_rows,
    output_gradient_rows,
    adapter_up_weight,
    input_side_projection,
    rank_side_projection,
    lengths,
    program_output_index,
    targets,
):
    narrow_count = lax.axis_size("narrow")
    narrow_index = lax.axis_index("narrow")
    programs = lengths.shape[0]
    length = layer_input_rows.shape[0] // programs
    reduced_sums = jnp.dot(
        output_gradient_rows, adapter_up_weight, preferred_element_type=jnp.float32
    )
    out_part = jnp.dot(
        reduced_sums, rank_side_projection.astype(jnp.float32), precision=lax.Precision.HIGHEST
    )
    in_part = jnp.dot(layer_input_rows, input_side_projection, preferred_element_type=jnp.float32)
    target_wide = targets.astype(jnp.float32)
    target_squares = jnp.sum(target_wide * target_wide, axis=1)
    out_all, in_all = (
        lax.psum(out_part.astype(jnp.bfloat16), "narrow").astype(jnp.float32),
        lax.psum(in_part.astype(jnp.bfloat16), "narrow").astype(jnp.float32),
    )
    quarter_cols = out_all.shape[1] // narrow_count
    quarter = lax.dynamic_slice_in_dim(out_all, narrow_index * quarter_cols, quarter_cols, 1)
    features = program_features(quarter, in_all, lengths, length)
    squares = jnp.sum(features * features, axis=1)
    squares, target_squares = lax.psum((squares, target_squares), "narrow")
    unit_rows = normalize_rows(features, squares)
    target_unit = normalize_rows(target_wide, target_squares)
    row_order = jnp.argsort(program_output_index)
    contract = (((1,), (1,)), ((), ()))
    root_count = math.sqrt(float(targets.shape[1] * narrow_count))
    gathered = lax.all_gather(unit_rows, "wide", axis=0, tiled=True)
    permuted = jnp.take(gathered, row_order, axis=0)
    summed = lax.psum_scatter(
        lax.dot_general(permuted, target_unit, contract, preferred_element_type=jnp.float32).astype(
            jnp.bfloat16
        ),
        "narrow",
        scatter_dimension=0,
        tiled=True,
    ).astype(jnp.float32)
    return summed * root_count


def solution(mesh):
    return jax.shard_map(
        shards,
        mesh=mesh,
        in_specs=(
            P("wide", "narrow"),
            P("wide", "narrow"),
            P("narrow", None),
            P("narrow", None),
            P(),
            P("wide"),
            P(),
            P("wide", "narrow"),
        ),
        out_specs=P("narrow", "wide"),
        check_vma=False,
    )
```

profile of v0, /device:TPU:1, one launch (start us, length us, event | category | flops | bytes accessed | tf_op | source)
XLA Modules:
  0.0 268.1 jit_solution(4653821214865068654)
XLA Ops:
  6.5 0.0 copy-start
  6.5 0.0 copy-start.1
  6.5 0.0 copy-start.3
  6.5 0.0 all-reduce.4.cloned.1.call-start
  6.5 0.9 copy-done
  7.5 4.2 %convolution_convert_fusion = bf16[2048,128]{1,0:T(8,128)(2,1)} fusion(bf16[2048,1024]{1,0:T(8,128)(2,1)} %param.8, bf16[1024,128]{1,0:T(8,128)(2,1)S(1)} %copy-done), kind=kOutput, calls=%fused_computation.12 | convolution fusion | flops 537133056 | bytes 4980736 | tf_op jit(solution)/shard_map/dot_general | solution.py:44
  11.7 3.5 %fusion.19 = f32[2048,128]{1,0:T(8,128)S(1)} fusion(bf16[2048,1024]{1,0:T(8,128)(2,1)} %param.9, bf16[1024,128]{1,0:T(8,128)(2,1)} %param.10), kind=kOutput, calls=%fused_computation.29 | convolution fusion | flops 536870912 | bytes 5505024 | tf_op jit(solution)/shard_map/dot_general | solution.py:38
  15.2 0.0 copy-done.1
  15.2 0.0 copy-start.2
  15.2 1.5 convolution_convert_fusion.1
  16.7 0.0 all-reduce.4.cloned.1.call-update
  16.7 0.0 all-gather.2.cloned.1.call-start
  16.8 0.0 copy-done.3
  16.8 0.1 fusion.16
  16.8 5.1 %fusion = f32[2048]{0:T(1024)S(1)} fusion(bf16[2048,2048]{1,0:T(8,128)(2,1)} %param.15), kind=kLoop, calls=%fused_computation.3 | loop fusion | flops 12580864 | bytes 8396800 | tf_op jit(solution)/shard_map/reduce_sum | solution.py:46
  21.9 40.8 %all-reduce.4.cloned.1.call-done = (bf16[64,32,128]{2,1,0:T(8,128)(2,1)}, bf16[2048,64]{0,1:T(8,128)(2,1)}) async-done(((bf16[64,32,128]{2,1,0:T(8,128)(2,1)}, bf16[2048,64]{0,1:T(8,128)(2,1)}), (bf16[64,32,128]{2,1,0:T(8,128)(2,1)}, bf16[2048,64]{0,1:T(8,128)(2,1)})) %all-reduce.4.cloned.1.call-update) | async-done | bytes 786448 | tf_op jit(solution)/shard_map/psum | solution.py:49
  62.8 0.8 dynamic-slice_convert_fusion
  63.6 0.2 reshape.36
  63.8 2.3 multiply_reduce_fusion
  66.1 8.2 %all-reduce = (f32[2048]{0:T(1024)S(1)}, f32[64]{0:T(128)S(1)}) all-reduce(f32[2048]{0:T(1024)S(1)} %fusion, f32[64]{0:T(128)S(1)} %get-tuple-element.11), channel_id=1, replica_groups=mesh['wide'=32,'narrow'=4] {'narrow'}, use_global_device_ids=true, to_apply=%region_6.0 | all-reduce | flops 2112 | bytes 16896 | tf_op jit(solution)/shard_map/psum | solution.py:55
  74.4 0.9 fusion.13
  75.3 0.0 all-gather.2.cloned.1.call-update
  75.3 0.2 reduce-scatter.2.cloned.1.call-start
  75.5 0.0 copy-done.2
  75.5 5.0 %sort.17 = (s32[2048]{0:T(1024)}, s32[2048]{0:T(1024)S(1)}) sort(s32[2048]{0:T(1024)S(1)} %copy-done.2, s32[2048]{0:T(1024)S(1)} %iota.11), dimensions={0}, to_apply=%region_0.0 | sort | flops 22528 | bytes 32768 | tf_op jit(solution)/shard_map/jit(argsort)/sort | solution.py:58
  80.6 50.8 %all-gather.2.cloned.1.call-done = bf16[2048,2048]{1,0:T(8,128)(2,1)} async-done(((bf16[64,2048]{1,0:T(8,128)(2,1)}), bf16[2048,2048]{1,0:T(8,128)(2,1)}) %all-gather.2.cloned.1.call-update) | async-done | bytes 8388624 | tf_op jit(solution)/shard_map/all_gather | solution.py:61
  131.4 20.8 %gather_fusion = bf16[2048,2048]{1,0:T(8,128)(2,1)} fusion(bf16[2048,2048]{1,0:T(8,128)(2,1)} %all-gather.2.cloned.1.call-done, s32[2048]{0:T(1024)S(1)} %fusion.17), kind=kCustom, calls=%fused_computation | custom fusion | bytes 16785408 | tf_op jit(solution)/shard_map/jit(_take)/gather | solution.py:62
  152.2 25.4 %fusion.7 = bf16[2048,2048]{1,0:T(8,128)(2,1)} fusion(bf16[2048,2048]{1,0:T(8,128)(2,1)} %param.15, f32[2048]{0:T(1024)S(1)} %add_rsqrt_fusion, bf16[2048,2048]{1,0:T(8,128)(2,1)} %gather_fusion, pred[2048]{0:T(1024)(128)(4,1)S(1)} %compare_and_fusion), kind=kOutput, calls=%fused_computation.9 | convolution fusion | flops 17200840704 | bytes 25176064 | tf_op jit(solution)/shard_map/dot_general | solution.py:64
  177.6 0.0 reduce-scatter.2.cloned.1.call-update
  177.6 79.8 %reduce-scatter.2.cloned.1.call-done = bf16[512,2048]{1,0:T(8,128)(2,1)} async-done(((bf16[2048,2048]{1,0:T(8,128)(2,1)}), bf16[512,2048]{1,0:T(8,128)(2,1)}) %reduce-scatter.2.cloned.1.call-update) | async-done | bytes 2097168 | tf_op jit(solution)/shard_map/reduce_scatter | solution.py:63
  257.4 4.2 %convert_multiply_fusion.2 = f32[512,2048]{1,0:T(8,128)} fusion(bf16[512,2048]{1,0:T(8,128)(2,1)} %reduce-scatter.2.cloned.1.call-done), kind=kLoop, calls=%fused_computation.10 | loop fusion | flops 2097152 | bytes 6291456 | tf_op jit(solution)/shard_map/mul | solution.py:71
  (6 shorter events, 0.1 us)
Async XLA Ops:
  6.5 1.0 copy-start
  6.5 8.7 %copy-start.1 = (bf16[128,64]{0,1:T(8,128)(2,1)S(1)}, bf16[128,64]{0,1:T(8,128)(2,1)}, u32[]{:S(2)}) copy-start(bf16[128,64]{0,1:T(8,128)(2,1)} %param.12) | copy-start | bytes 49156
  6.5 10.2 %copy-start.3 = (s32[64]{0:T(128)S(1)}, s32[64]{0:T(128)}, u32[]{:S(2)}) copy-start(s32[64]{0:T(128)} %param.13) | copy-start | bytes 772
  6.5 56.2 %all-reduce.4.cloned.1.call-start = ((), (), s32[]{:S(2)}) async-start(), calls=%async_computation.3 | async-start | bytes 1572864 | tf_op jit(solution)/shard_map/psum | solution.py:49
  15.2 60.3 %copy-start.2 = (s32[2048]{0:T(1024)S(1)}, s32[2048]{0:T(1024)}, u32[]{:S(2)}) copy-start(s32[2048]{0:T(1024)} %param.14) | copy-start | bytes 24580
  16.7 114.7 %all-gather.2.cloned.1.call-start = ((), (), s32[]{:S(2)}) async-start(), calls=%async_computation.1 | async-start | bytes 8650752 | tf_op jit(solution)/shard_map/all_gather | solution.py:61
  75.3 182.1 %reduce-scatter.2.cloned.1.call-start = ((), (), s32[]{:S(2)}) async-start(), calls=%async_computation.2 | async-start | bytes 10485760 | tf_op jit(solution)/shard_map/reduce_scatter | solution.py:63
Sparse Core Ops, SparseCore 0:
  16.8 45.8 all-reduce.3
  75.4 55.9 all-gather.1
  177.8 79.5 reduce-scatter.1
where the time goes:
time: 268 us
  waiting for transfers between devices  171 us (64%)
  matrix products  36.8 us (14%)
  local copies, waits for them, and re-layouts  21.9 us (8%)
  other arithmetic  16.2 us (6%)
  between operations  13.2 us (5%)
  blocking collectives  8.25 us (3%)
    reduce_scatter x1, waiting for transfers between devices, shards(): lax.psum_scatter(lax.dot_general(permuted, target_unit, contract, preferr...  79.8 us
    all_gather x1, waiting for transfers between devices, shards(): gathered = lax.all_gather(unit_rows, 'wide', axis=0, tiled=True)  50.8 us
    psum x1, waiting for transfers between devices, shards(): lax.psum(in_part.astype(jnp.bfloat16), 'narrow').astype(jnp.float32)  40.8 us
    dot_general x1, matrix products, shards(): lax.dot_general(permuted, target_unit, contract, preferred_element_type=j...  25.4 us
    gather x1, local copies, waits for them, and re-layouts, shards(): permuted = jnp.take(gathered, row_order, axis=0)  20.8 us
    psum x1, blocking collectives, shards(): squares, target_squares = lax.psum((squares, target_squares), 'narrow')  8.25 us
  transfers between devices with their start and end apart: 3, of which 3 were waited for; matrix products, arithmetic and copies ran while one was open for 4% of the time, Pallas kernels for 0%

commit v1 on v0

--- a/solution.py
+++ b/solution.py
@@ -58,7 +58,8 @@
     row_order = jnp.argsort(program_output_index)
     contract = (((1,), (1,)), ((), ()))
     root_count = math.sqrt(float(targets.shape[1] * narrow_count))
-    gathered = lax.all_gather(unit_rows, "wide", axis=0, tiled=True)
+    stack = jnp.stack([unit_rows] * lax.axis_size("wide"))
+    gathered = jnp.concatenate(lax.all_to_all(stack, "wide", 0, 0), axis=0)
     permuted = jnp.take(gathered, row_order, axis=0)
     summed = lax.psum_scatter(
         lax.dot_general(permuted, target_unit, contract, preferred_element_type=jnp.float32).astype(

time: 268 us -> 350 us (1.31)
  waiting for transfers between devices: 171 us -> 238 us
  starting transfers between devices: 0.27 us -> 11.5 us
  local copies, waits for them, and re-layouts: 21.9 us -> 26.2 us
    all_to_all x0 -> x1, waiting for transfers between devices: none -> 103 us  [shards(): gathered = jnp.concatenate(lax.all_to_all(stack, 'wide', 0, 0), axis=0)]
    all_gather x1 -> x0, waiting for transfers between devices: 50.8 us -> none  [shards(): gathered = lax.all_gather(unit_rows, 'wide', axis=0, tiled=True)]
    reduce_scatter x1, waiting for transfers between devices: 79.8 us -> 93.5 us  [shards(): lax.psum_scatter(lax.dot_general(permuted, target_unit, contract, preferr...]
    all_to_all x0 -> x1, starting transfers between devices: none -> 11.2 us  [shards(): gathered = jnp.concatenate(lax.all_to_all(stack, 'wide', 0, 0), axis=0)]
    another operation x0 -> x1, local copies, waits for them, and re-layouts: none -> 4.28 us  [shards(): stack = jnp.stack([unit_rows] * lax.axis_size('wide'))]
  transfers between devices with their start and end apart: 3 -> 3, of which waited for: 3 -> 3; matrix products, arithmetic and copies ran while one was open for 4% -> 3% of each run, Pallas kernels for 0% -> 0%
where the time goes in v1:
time: 350 us; the launch traced here: 349 us
  waiting for transfers between devices  238 us (68%)
  matrix products  36.8 us (11%)
  local copies, waits for them, and re-layouts  26.2 us (7%)
  other arithmetic  15.5 us (4%)
  between operations  13.5 us (4%)
  starting transfers between devices  11.5 us (3%)
  blocking collectives  8.25 us (2%)
    all_to_all x1, waiting for transfers between devices, shards(): gathered = jnp.concatenate(lax.all_to_all(stack, 'wide', 0, 0), axis=0)  103 us
    reduce_scatter x1, waiting for transfers between devices, shards(): lax.psum_scatter(lax.dot_general(permuted, target_unit, contract, preferr...  93.5 us
    psum x1, waiting for transfers between devices, shards(): lax.psum(in_part.astype(jnp.bfloat16), 'narrow').astype(jnp.float32)  40.9 us
    dot_general x1, matrix products, shards(): lax.dot_general(permuted, target_unit, contract, preferred_element_type=j...  25.4 us
    gather x1, local copies, waits for them, and re-layouts, shards(): permuted = jnp.take(gathered, row_order, axis=0)  20.8 us
    all_to_all x1, starting transfers between devices, shards(): gathered = jnp.concatenate(lax.all_to_all(stack, 'wide', 0, 0), axis=0)  11.2 us
    psum x1, blocking collectives, shards(): squares, target_squares = lax.psum((squares, target_squares), 'narrow')  8.25 us
  transfers between devices with their start and end apart: 3, of which 3 were waited for; matrix products, arithmetic and copies ran while one was open for 3% of the time, Pallas kernels for 0%

profile of v1, /device:TPU:1, one launch (start us, length us, event | category | flops | bytes accessed | tf_op | source)
XLA Modules:
  0.0 349.4 jit_solution(583768007779534158)
XLA Ops:
  6.5 0.0 copy-start
  6.5 0.0 copy-start.1
  6.5 0.0 copy-start.3
  6.5 0.0 all-reduce.4.cloned.1.call-start
  6.5 0.9 copy-done
  7.5 4.2 %convolution_convert_fusion = bf16[2048,128]{1,0:T(8,128)(2,1)} fusion(bf16[2048,1024]{1,0:T(8,128)(2,1)} %param.8, bf16[1024,128]{1,0:T(8,128)(2,1)S(1)} %copy-done), kind=kOutput, calls=%fused_computation.12 | convolution fusion | flops 537133056 | bytes 4980736 | tf_op jit(solution)/shard_map/dot_general | solution.py:44
  11.7 3.5 fusion.19
  15.2 0.0 copy-done.1
  15.2 1.5 convolution_convert_fusion.1
  16.7 0.0 all-reduce.4.cloned.1.call-update
  16.7 0.0 copy-done.3
  16.7 0.1 fusion.16
  16.8 5.1 %fusion = f32[2048]{0:T(1024)S(1)} fusion(bf16[2048,2048]{1,0:T(8,128)(2,1)} %param.15), kind=kLoop, calls=%fused_computation.3 | loop fusion | flops 12580864 | bytes 8396800 | tf_op jit(solution)/shard_map/reduce_sum | solution.py:46
  21.9 40.9 %all-reduce.4.cloned.1.call-done = (bf16[64,32,128]{2,1,0:T(8,128)(2,1)}, bf16[2048,64]{0,1:T(8,128)(2,1)}) async-done(((bf16[64,32,128]{2,1,0:T(8,128)(2,1)}, bf16[2048,64]{0,1:T(8,128)(2,1)}), (bf16[64,32,128]{2,1,0:T(8,128)(2,1)}, bf16[2048,64]{0,1:T(8,128)(2,1)})) %all-reduce.4.cloned.1.call-update) | async-done | bytes 786448 | tf_op jit(solution)/shard_map/psum | solution.py:49
  62.8 0.8 dynamic-slice_convert_fusion
  63.6 0.2 reshape.48
  63.8 2.3 multiply_reduce_fusion
  66.1 8.2 %all-reduce = (f32[2048]{0:T(1024)S(1)}, f32[64]{0:T(128)S(1)}) all-reduce(f32[2048]{0:T(1024)S(1)} %fusion, f32[64]{0:T(128)S(1)} %get-tuple-element.11), channel_id=1, replica_groups=mesh['wide'=32,'narrow'=4] {'narrow'}, use_global_device_ids=true, to_apply=%region_6.0 | all-reduce | flops 2112 | bytes 16896 | tf_op jit(solution)/shard_map/psum | solution.py:55
  74.4 0.2 fusion.13
  74.6 4.3 %stack.2 = bf16[32,64,2048]{2,1,0:T(8,128)(2,1)} broadcast(bf16[64,2048]{1,0:T(8,128)(2,1)S(1)} %fusion.13), dimensions={1,2} | broadcast | bytes 8650752 | tf_op jit(solution)/shard_map/stack | solution.py:61
  78.8 0.0 copy-start.2
  78.8 11.2 %all-to-all-start = ((bf16[32,64,2048]{2,1,0:T(8,128)(2,1)}), bf16[32,64,2048]{2,1,0:T(8,128)(2,1)}, u32[]{:S(2)}, u32[]{:S(2)}) async-start(bf16[32,64,2048]{2,1,0:T(8,128)(2,1)} %stack.2), calls=%async_computation | async-start | bytes 16777216 | tf_op jit(solution)/shard_map/all_to_all | solution.py:62
  90.1 0.2 reduce-scatter.2.cloned.1.call-start
  90.3 0.0 copy-done.2
  90.3 5.0 %sort.17 = (s32[2048]{0:T(1024)}, s32[2048]{0:T(1024)S(1)}) sort(s32[2048]{0:T(1024)S(1)} %copy-done.2, s32[2048]{0:T(1024)S(1)} %iota.11), dimensions={0}, to_apply=%region_0.0 | sort | flops 22528 | bytes 32768 | tf_op jit(solution)/shard_map/jit(argsort)/sort | solution.py:58
  95.4 103.2 %all-to-all-done = bf16[32,64,2048]{2,1,0:T(8,128)(2,1)} async-done(((bf16[32,64,2048]{2,1,0:T(8,128)(2,1)}), bf16[32,64,2048]{2,1,0:T(8,128)(2,1)}, u32[]{:S(2)}, u32[]{:S(2)}) %all-to-all-start) | async-done | bytes 8388640 | tf_op jit(solution)/shard_map/all_to_all | solution.py:62
  198.6 20.8 %gather_fusion = bf16[2048,2048]{1,0:T(8,128)(2,1)} fusion(bf16[2048,2048]{1,0:T(8,128)(2,1)} %bitcast.1, s32[2048]{0:T(1024)S(1)} %fusion.17), kind=kCustom, calls=%fused_computation | custom fusion | bytes 16785408 | tf_op jit(solution)/shard_map/jit(_take)/gather | solution.py:63
  219.4 25.4 %fusion.7 = bf16[2048,2048]{1,0:T(8,128)(2,1)} fusion(bf16[2048,2048]{1,0:T(8,128)(2,1)} %param.15, f32[2048]{0:T(1024)S(1)} %add_rsqrt_fusion, bf16[2048,2048]{1,0:T(8,128)(2,1)} %gather_fusion, pred[2048]{0:T(1024)(128)(4,1)S(1)} %compare_and_fusion), kind=kOutput, calls=%fused_computation.9 | convolution fusion | flops 17200840704 | bytes 25176064 | tf_op jit(solution)/shard_map/dot_general | solution.py:65
  244.8 0.0 reduce-scatter.2.cloned.1.call-update
  244.8 93.5 %reduce-scatter.2.cloned.1.call-done = bf16[512,2048]{1,0:T(8,128)(2,1)} async-done(((bf16[2048,2048]{1,0:T(8,128)(2,1)}), bf16[512,2048]{1,0:T(8,128)(2,1)}) %reduce-scatter.2.cloned.1.call-update) | async-done | bytes 2097168 | tf_op jit(solution)/shard_map/reduce_scatter | solution.py:64
  338.4 4.2 %convert_multiply_fusion.2 = f32[512,2048]{1,0:T(8,128)} fusion(bf16[512,2048]{1,0:T(8,128)(2,1)} %reduce-scatter.2.cloned.1.call-done), kind=kLoop, calls=%fused_computation.10 | loop fusion | flops 2097152 | bytes 6291456 | tf_op jit(solution)/shard_map/mul | solution.py:72
  (6 shorter events, 0.1 us)
Async XLA Ops:
  6.5 1.0 copy-start
  6.5 8.7 %copy-start.1 = (bf16[128,64]{0,1:T(8,128)(2,1)S(1)}, bf16[128,64]{0,1:T(8,128)(2,1)}, u32[]{:S(2)}) copy-start(bf16[128,64]{0,1:T(8,128)(2,1)} %param.12) | copy-start | bytes 49156
  6.5 10.2 %copy-start.3 = (s32[64]{0:T(128)S(1)}, s32[64]{0:T(128)}, u32[]{:S(2)}) copy-start(s32[64]{0:T(128)} %param.13) | copy-start | bytes 772
  6.5 56.2 %all-reduce.4.cloned.1.call-start = ((), (), s32[]{:S(2)}) async-start(), calls=%async_computation.3 | async-start | bytes 1572864 | tf_op jit(solution)/shard_map/psum | solution.py:49
  78.8 11.5 %copy-start.2 = (s32[2048]{0:T(1024)S(1)}, s32[2048]{0:T(1024)}, u32[]{:S(2)}) copy-start(s32[2048]{0:T(1024)} %param.14) | copy-start | bytes 24580
  78.8 119.8 %all-to-all-start = ((bf16[32,64,2048]{2,1,0:T(8,128)(2,1)}), bf16[32,64,2048]{2,1,0:T(8,128)(2,1)}, u32[]{:S(2)}, u32[]{:S(2)}) async-start(bf16[32,64,2048]{2,1,0:T(8,128)(2,1)} %stack.2), calls=%async_computation | async-start | bytes 16777216 | tf_op jit(solution)/shard_map/all_to_all | solution.py:62
  90.1 248.3 %reduce-scatter.2.cloned.1.call-start = ((), (), s32[]{:S(2)}) async-start(), calls=%async_computation.2 | async-start | bytes 10485760 | tf_op jit(solution)/shard_map/reduce_scatter | solution.py:64
Sparse Core Ops, SparseCore 0:
  16.8 45.8 all-reduce.3
  245.0 93.3 reduce-scatter.1
